TPU v7x, 32 devices: a whole 2x2x4 slice. The times are simulated.
32 devices in a mesh: dp: 4 (over x, core), group: 8 (over z, y).
Axes of the slice: x: 2, y: 2, z: 4, core: 2. Of those that a mesh axis runs over, the one named last changes fastest.
Arguments:
- features: bfloat16 [8192, 3072], P(('dp', 'group')), may hold values from -6 to 6
- target_embed: bfloat16 [8192, 256], P(('dp', 'group')), may hold values from -80 to 80
- proj_weight: bfloat16 [3072, 256], replicated, may hold values from -0.109375 to 0.109375
- prototypes: float32 [2048, 256], replicated, may hold values from -20 to 20
Outputs:
- grad_feat: bfloat16 [8192, 3072], P(('dp', 'group'))
- grad_proj: float32 [3072, 256], P('group')
- grad_protos: float32 [2048, 256], replicated
All inputs are finite; a program needn't handle non-finite values.
Results may differ from a plain program's by a relative error of at most 0.0067.
Values sent between devices are 32-bit elements; how exact they have to be, the bound alone decides.
A program may use at most 64 MiB of HBM per device.

v0:
```python
import jax
import jax.numpy as jnp
from jax import lax
from jax.sharding import PartitionSpec as P

SWEEPS = 3


def normalize(values):
    return values * lax.rsqrt(jnp.sum(values * values, axis=-1, keepdims=True) + 1e-06)


def rownorm(matrix):
    return matrix / jnp.sum(matrix, axis=1, keepdims=True)


def column_total(partial_value):
    return lax.psum(partial_value, ("dp", "group"))


def local(features, target_embed, proj_weight, prototypes):
    unit_protos, proto_back = jax.vjp(normalize, prototypes)
    proto_b = unit_protos.astype(jnp.bfloat16)
    target_b = normalize(target_embed.astype(jnp.float32)).astype(jnp.bfloat16)
    scores = jnp.dot(target_b, proto_b.T, preferred_element_type=jnp.float32)
    plan = rownorm(jnp.exp(scores * (1.0 / 0.05)))
    for sweep in range(SWEEPS):
        colsum = column_total(jnp.sum(plan, axis=0))
        plan = rownorm(plan / colsum)
    hidden = jnp.dot(features, proj_weight, preferred_element_type=jnp.float32)
    embed, embed_back = jax.vjp(normalize, hidden)
    embed_b = embed.astype(jnp.bfloat16)
    online = jnp.dot(embed_b, proto_b.T, preferred_element_type=jnp.float32)
    prob = jax.nn.softmax(online * (1.0 / 0.1), axis=1)
    grad_scores = ((prob - plan) * (1.0 / 0.1)).astype(jnp.bfloat16)
    local_unit = lax.dot_general(
        grad_scores, embed_b, (((0,), (0,)), ((), ())), preferred_element_type=jnp.float32
    )
    grad_unit = lax.psum(local_unit, ("dp", "group"))
    grad_protos = proto_back(grad_unit)[0]
    grad_embed = jnp.dot(grad_scores, proto_b, preferred_element_type=jnp.float32)
    grad_hidden = embed_back(grad_embed)[0].astype(jnp.bfloat16)
    grad_feat = lax.dot_general(
        grad_hidden, proj_weight, (((1,), (1,)), ((), ())), preferred_element_type=jnp.float32
    ).astype(jnp.bfloat16)
    grad_part = lax.psum_scatter(
        lax.dot_general(
            features, grad_hidden, (((0,), (0,)), ((), ())), preferred_element_type=jnp.float32
        ),
        "group",
        scatter_dimension=0,
        tiled=True,
    )
    grad_proj = lax.psum(grad_part, "dp")
    return (grad_feat, grad_proj, grad_protos)


def solution(mesh):
    return jax.shard_map(
        local,
        mesh=mesh,
        in_specs=(P(("dp", "group"), None), P(("dp", "group"), None), P(), P()),
        out_specs=(P(("dp", "group"), None), P("group", None), P()),
        check_vma=False,
    )
```

profile of v0, /device:TPU:0, one launch (start us, length us, event | category | flops | bytes accessed | tf_op | source)
XLA Modules:
  0.0 346.1 jit_solution(14579434763321458965)
XLA Ops:
  8.0 0.0 copy-start
  8.0 0.0 all-reduce.5.cloned.1.call-start
  8.1 0.0 copy-start.5
  8.1 2.1 multiply_reduce_fusion.1
  10.2 0.0 copy-start.9
  10.2 0.2 copy-done.5
  10.4 0.3 multiply_convert_fusion.1
  10.7 0.4 copy-done.9
  11.1 0.1 fusion.17
  11.3 0.6 fusion.23
  11.8 0.0 copy-start.1
  11.8 1.3 copy-done.1
  13.2 0.3 divide_reduce_fusion
  13.5 42.1 %psum.35 = f32[2048]{0:T(1024)S(1)} all-reduce(f32[2048]{0:T(1024)S(1)} %divide_reduce_fusion), channel_id=1, replica_groups=mesh['dp'=4,'group'=8] {'dp','group'}, use_global_device_ids=true, to_apply=%region_7.0 | all-reduce | flops 2048 | bytes 16384 | tf_op jit(solution)/shard_map/psum | solution.py:18
  55.6 2.2 fusion.11
  57.7 0.1 copy-done.2
  57.8 0.4 fusion.12
  58.2 40.2 %psum.36 = f32[2048]{0:T(1024)S(1)} all-reduce(f32[2048]{0:T(1024)S(1)} %fusion.12), channel_id=1, replica_groups=mesh['dp'=4,'group'=8] {'dp','group'}, use_global_device_ids=true, to_apply=%region_10.0 | all-reduce | flops 2048 | bytes 16384 | tf_op jit(solution)/shard_map/psum | solution.py:18
  98.5 2.3 fusion.13
  100.8 0.0 copy-done.3
  100.8 0.7 fusion.14
  101.4 40.1 %psum.37 = f32[2048]{0:T(1024)S(1)} all-reduce(f32[2048]{0:T(1024)S(1)} %fusion.14), channel_id=1, replica_groups=mesh['dp'=4,'group'=8] {'dp','group'}, use_global_device_ids=true, to_apply=%region_13.0 | all-reduce | flops 2048 | bytes 16384 | tf_op jit(solution)/shard_map/psum | solution.py:18
  141.5 2.4 fusion.15
  143.9 0.0 copy-done
  144.0 0.8 multiply_reduce_fusion.3
  144.8 0.0 copy-start.4
  144.8 0.6 fusion.24
  145.3 0.4 fusion.16
  145.8 0.6 copy-done.4
  146.4 1.4 multiply_convert_fusion
  147.7 0.0 copy-start.6
  147.8 1.0 copy-done.6
  148.7 1.8 fusion.22
  150.5 0.0 all-reduce.5.cloned.1.call-update
  150.6 0.0 reduce-scatter.2.cloned.1.call-start
  150.6 1.8 multiply_reduce_fusion.2
  152.4 2.2 convolution_bitcast_fusion
  154.7 0.0 reduce-scatter.2.cloned.1.call-update
  154.7 0.0 all-reduce.3.cloned.1.call-start
  154.8 1.4 copy-done.8
  156.2 1.8 convolution_convert_fusion
  158.0 144.7 %all-reduce.5.cloned.1.call-done = f32[2048,256]{1,0:T(8,128)} async-done(((f32[2048,256]{1,0:T(8,128)}), f32[2048,256]{1,0:T(8,128)}) %all-reduce.5.cloned.1.call-update) | async-done | bytes 2097168 | tf_op jit(solution)/shard_map/psum | solution.py:39
  302.6 2.6 multiply_reduce_fusion
  305.2 0.0 reduce-scatter.2.cloned.1.call-done
  305.3 0.0 all-reduce.3.cloned.1.call-update
  305.3 3.5 %add_add_fusion = f32[2048,256]{1,0:T(8,128)} fusion(f32[2048,256]{1,0:T(8,128)} %param.7, f32[2048,256]{1,0:T(8,128)} %all-reduce.5.cloned.1.call-done, f32[2048]{0:T(1024)S(1)} %multiply_multiply_fusion.1, f32[2048]{0:T(1024)S(1)} %add_rsqrt_fusion), kind=kLoop, calls=%fused_computation.2 | loop fusion | flops 2097152 | bytes 6307840 | tf_op jit(solution)/shard_map/transpose(jvp())/add_any | solution.py:10
  308.8 28.0 %all-reduce.3.cloned.1.call-done = f32[384,256]{0,1:T(8,128)} async-done(((f32[384,256]{0,1:T(8,128)}), f32[384,256]{0,1:T(8,128)}) %all-reduce.3.cloned.1.call-update) | async-done | bytes 393232 | tf_op jit(solution)/shard_map/psum | solution.py:54
  336.7 1.9 copy.7
  (11 shorter events, 0.1 us)
Async XLA Ops:
  8.0 136.0 %copy-start = (bf16[256,3072]{1,0:T(8,128)(2,1)S(1)}, bf16[256,3072]{1,0:T(8,128)(2,1)}, u32[]{:S(2)}) copy-start(bf16[256,3072]{1,0:T(8,128)(2,1)} %param.4) | copy-start | bytes 4718596
  8.0 294.6 %all-reduce.5.cloned.1.call-start = ((), (), s32[]{:S(2)}) async-start(), calls=%async_computation.3 | async-start | bytes 4194304 | tf_op jit(solution)/shard_map/psum | solution.py:39
  8.1 2.3 copy-start.5
  10.2 1.0 copy-start.9
  11.8 1.3 copy-start.1
  55.6 2.2 copy-start.2
  98.5 2.3 copy-start.3
  141.5 2.4 copy-start.7
  144.8 1.6 copy-start.4
  147.7 1.0 copy-start.6
  150.6 154.7 %reduce-scatter.2.cloned.1.call-start = ((), (), s32[]{:S(2)}) async-start(), calls=%async_computation.1 | async-start | bytes 3538944 | tf_op jit(solution)/shard_map/reduce_scatter | solution.py:46
  154.7 1.5 copy-start.8
  154.7 182.0 %all-reduce.3.cloned.1.call-start = ((), (), s32[]{:S(2)}) async-start(), calls=%async_computation.2 | async-start | bytes 786432 | tf_op jit(solution)/shard_map/psum | solution.py:54
Sparse Core Ops, SparseCore 0:
  150.7 151.9 all-reduce.4
Sparse Core Ops, SparseCore 1:
  154.8 82.1 reduce-scatter.1
  305.4 31.3 all-reduce.2
where the time goes:
time: 347 us; the launch traced here: 346 us
  waiting for transfers between devices  173 us (50%)
  blocking collectives  122 us (35%)
  other arithmetic  18.8 us (5%)
  between operations  15.7 us (5%)
  matrix products  9.52 us (3%)
  local copies, waits for them, and re-layouts  6.88 us (2%)
    psum x1, waiting for transfers between devices, local(): grad_unit = lax.psum(local_unit, ('dp', 'group'))  145 us
    psum x3, blocking collectives, column_total(): return lax.psum(partial_value, ('dp', 'group'))  122 us
    psum x1, waiting for transfers between devices, local(): grad_proj = lax.psum(grad_part, 'dp')  28 us
  transfers between devices with their start and end apart: 3, of which 2 were waited for; matrix products, arithmetic and copies ran while one was open for 3% of the time, Pallas kernels for 0%

commit v1 on v0

--- a/solution.py
+++ b/solution.py
@@ -36,7 +36,7 @@
     local_unit = lax.dot_general(
         grad_scores, embed_b, (((0,), (0,)), ((), ())), preferred_element_type=jnp.float32
     )
-    grad_unit = lax.psum(local_unit, ("dp", "group"))
+    grad_unit = lax.psum(lax.psum(local_unit, "group"), "dp")
     grad_protos = proto_back(grad_unit)[0]
     grad_embed = jnp.dot(grad_scores, proto_b, preferred_element_type=jnp.float32)
     grad_hidden = embed_back(grad_embed)[0].astype(jnp.bfloat16)

time: 347 us -> 402 us (1.16)
  waiting for transfers between devices: 173 us -> 233 us
    reduce_scatter x1, waiting for transfers between devices: 0.03 us -> 77.6 us  [local(): lax.psum_scatter(lax.dot_general(features, grad_hidden, (((0,), (0,)), ((...]
    psum x1, waiting for transfers between devices: 145 us -> 97.6 us  [local(): grad_unit = lax.psum(lax.psum(local_unit, 'group'), 'dp')]
    psum x1, waiting for transfers between devices: 28 us -> 57.7 us  [local(): grad_proj = lax.psum(grad_part, 'dp')]
  transfers between devices with their start and end apart: 3 -> 3, of which waited for: 2 -> 3; matrix products, arithmetic and copies ran while one was open for 3% -> 1% of each run, Pallas kernels for 0% -> 0%
where the time goes in v1:
time: 402 us; the launch traced here: 401 us
  waiting for transfers between devices  233 us (58%)
  blocking collectives  122 us (30%)
  other arithmetic  17.1 us (4%)
  between operations  13.9 us (3%)
  matrix products  9.52 us (2%)
  local copies, waits for them, and re-layouts  5.2 us (1%)
    psum x3, blocking collectives, column_total(): return lax.psum(partial_value, ('dp', 'group'))  122 us
    psum x1, waiting for transfers between devices, local(): grad_unit = lax.psum(lax.psum(local_unit, 'group'), 'dp')  97.6 us
    reduce_scatter x1, waiting for transfers between devices, local(): lax.psum_scatter(lax.dot_general(features, grad_hidden, (((0,), (0,)), ((...  77.6 us
    psum x1, waiting for transfers between devices, local(): grad_proj = lax.psum(grad_part, 'dp')  57.7 us
  transfers between devices with their start and end apart: 3, of which 3 were waited for; matrix products, arithmetic and copies ran while one was open for 1% of the time, Pallas kernels for 0%

profile of v1, /device:TPU:0, one launch (start us, length us, event | category | flops | bytes accessed | tf_op | source)
XLA Modules:
  0.0 401.1 jit_solution(93144885395573999)
XLA Ops:
  7.2 0.0 copy-start
  7.2 0.0 all-reduce.4.cloned.1.call-start
  7.2 0.0 copy-start.5
  7.2 2.1 multiply_reduce_fusion.1
  9.3 0.0 copy-start.11
  9.4 0.2 copy-done.5
  9.6 0.3 multiply_convert_fusion.1
  9.9 0.4 copy-done.11
  10.3 0.1 fusion.17
  10.4 0.6 fusion.23
  11.0 0.0 copy-start.1
  11.0 1.3 copy-done.1
  12.3 0.3 divide_reduce_fusion
  12.6 42.1 %psum.42 = f32[2048]{0:T(1024)S(1)} all-reduce(f32[2048]{0:T(1024)S(1)} %divide_reduce_fusion), channel_id=1, replica_groups=mesh['dp'=4,'group'=8] {'dp','group'}, use_global_device_ids=true, to_apply=%region_7.0 | all-reduce | flops 2048 | bytes 16384 | tf_op jit(solution)/shard_map/psum | solution.py:18
  54.7 2.2 fusion.11
  56.9 0.1 copy-done.2
  57.0 0.4 fusion.12
  57.4 40.2 %psum.43 = f32[2048]{0:T(1024)S(1)} all-reduce(f32[2048]{0:T(1024)S(1)} %fusion.12), channel_id=1, replica_groups=mesh['dp'=4,'group'=8] {'dp','group'}, use_global_device_ids=true, to_apply=%region_10.0 | all-reduce | flops 2048 | bytes 16384 | tf_op jit(solution)/shard_map/psum | solution.py:18
  97.6 2.3 fusion.13
  99.9 0.7 fusion.14
  100.6 40.1 %psum.44 = f32[2048]{0:T(1024)S(1)} all-reduce(f32[2048]{0:T(1024)S(1)} %fusion.14), channel_id=1, replica_groups=mesh['dp'=4,'group'=8] {'dp','group'}, use_global_device_ids=true, to_apply=%region_13.0 | all-reduce | flops 2048 | bytes 16384 | tf_op jit(solution)/shard_map/psum | solution.py:18
  140.7 2.4 fusion.15
  143.1 0.0 copy-done.9
  143.1 0.8 multiply_reduce_fusion.3
  143.9 0.0 copy-start.4
  143.9 0.6 fusion.24
  144.5 0.4 fusion.16
  144.9 0.6 copy-done.4
  145.5 1.4 multiply_convert_fusion
  146.9 0.0 copy-start.7
  146.9 1.0 copy-done.7
  147.9 1.8 fusion.22
  149.7 0.0 all-reduce.4.cloned.1.call-update
  149.7 0.0 reduce-scatter.2.cloned.1.call-start
  149.7 1.8 multiply_reduce_fusion.2
  151.6 2.2 convolution_bitcast_fusion
  153.8 0.0 reduce-scatter.2.cloned.1.call-update
  153.9 0.0 all-reduce.6.cloned.1.call-start
  153.9 97.6 %all-reduce.4.cloned.1.call-done = f32[2048,256]{1,0:T(8,128)} async-done(((f32[2048,256]{1,0:T(8,128)}), f32[2048,256]{1,0:T(8,128)}) %all-reduce.4.cloned.1.call-update) | async-done | bytes 2097168 | tf_op jit(solution)/shard_map/psum | solution.py:39
  251.5 77.6 %reduce-scatter.2.cloned.1.call-done = f32[384,256]{0,1:T(8,128)} async-done(((f32[3072,256]{0,1:T(8,128)}), f32[384,256]{0,1:T(8,128)}) %reduce-scatter.2.cloned.1.call-update) | async-done | bytes 393232 | tf_op jit(solution)/shard_map/reduce_scatter | solution.py:46
  329.1 0.0 all-reduce.6.cloned.1.call-update
  329.1 1.8 convolution_convert_fusion
  330.9 57.7 %all-reduce.6.cloned.1.call-done = (f32[384,256]{0,1:T(8,128)}, f32[2048,256]{1,0:T(8,128)}) async-done(((f32[384,256]{0,1:T(8,128)}, f32[2048,256]{1,0:T(8,128)}), (f32[384,256]{0,1:T(8,128)}, f32[2048,256]{1,0:T(8,128)})) %all-reduce.6.cloned.1.call-update) | async-done | bytes 2490384 | tf_op jit(solution)/shard_map/psum | solution.py:54
  388.6 2.7 multiply_reduce_fusion
  391.3 0.1 copy-done.6
  391.4 0.6 copy-done.8
  392.0 1.7 add_add_fusion
  393.7 0.9 copy.7
  (17 shorter events, 0.1 us)
Async XLA Ops:
  7.2 135.9 %copy-start = (bf16[256,3072]{1,0:T(8,128)(2,1)S(1)}, bf16[256,3072]{1,0:T(8,128)(2,1)}, u32[]{:S(2)}) copy-start(bf16[256,3072]{1,0:T(8,128)(2,1)} %param.4) | copy-start | bytes 4718596
  7.2 244.3 %all-reduce.4.cloned.1.call-start = ((), (), s32[]{:S(2)}) async-start(), calls=%async_computation.2 | async-start | bytes 4194304 | tf_op jit(solution)/shard_map/psum | solution.py:39
  7.2 2.3 copy-start.5
  9.3 1.0 copy-start.11
  11.0 1.3 copy-start.1
  54.7 2.2 copy-start.2
  97.6 2.3 copy-start.3
  140.7 2.4 copy-start.9
  143.9 1.6 copy-start.4
  146.9 1.0 copy-start.7
  149.7 179.4 %reduce-scatter.2.cloned.1.call-start = ((), (), s32[]{:S(2)}) async-start(), calls=%async_computation.1 | async-start | bytes 3538944 | tf_op jit(solution)/shard_map/reduce_scatter | solution.py:46
  153.8 175.3 %copy-start.10 = (bf16[3072,256]{1,0:T(8,128)(2,1)S(1)}, bf16[3072,256]{1,0:T(8,128)(2,1)}, u32[]{:S(2)}) copy-start(bf16[3072,256]{1,0:T(8,128)(2,1)} %param.6) | copy-start | bytes 4718596
  153.9 234.7 %all-reduce.6.cloned.1.call-start = ((), (), s32[]{:S(2)}) async-start(), calls=%async_computation.3 | async-start | bytes 4980736 | tf_op jit(solution)/shard_map/psum | solution.py:54
  388.6 2.9 copy-start.6
  388.6 3.5 copy-start.8
  392.0 1.7 copy-start.12
Sparse Core Ops, SparseCore 0:
  149.8 101.6 all-reduce.3
  255.1 73.9 reduce-scatter.1
  331.5 57.0 all-reduce.5
